TPU v7x, 512 devices: a whole 4x4x16 slice. The times are simulated.
512 devices in a mesh: row: 64 (over z, x_hi, core), rep: 8 (over y, x_lo).
Axes of the slice: x: 4 (x_hi: 2, x_lo: 2; x = x_hi * 2 + x_lo), y: 4, z: 16, core: 2. Of those that a mesh axis runs over, the one named last changes fastest.
Arguments:
- features: float32 [65536, 128], P(('row', 'rep')), may hold values from -6 to 6
- weight: float32 [128, 256], replicated, may hold values from -0.5 to 0.5
- bias: float32 [256], replicated, may hold values from -3 to 3
- adjacency: float32 [64, 8, 64, 128, 128], P('row', 'rep')
- tile_row: int32 [64, 8, 64], P('row', 'rep'), may hold values from 0 to 7
- tile_live: int32 [64, 8, 64], P('row', 'rep'), may hold values from 0 to 1
- node_live: int32 [65536], P(('row', 'rep')), may hold values 0 or 1
- cotangent: float32 [65536, 256], P(('row', 'rep'))
Outputs:
- activations: float32 [65536, 256], P(('row', 'rep'))
- weight_grad: float32 [128, 256], replicated
- bias_grad: float32 [256], replicated
All inputs are finite; a program needn't handle non-finite values. No bound on the sum of `node_live` on one device may be relied on, other than what follows from the above.
Results may differ from a plain program's by a relative error of at most 0.0003.
Values sent between devices are 32-bit elements; how exact they have to be, the bound alone decides.
A program may use at most 64 MiB of HBM per device.

v0:
```python
import jax
import jax.numpy as jnp
from jax import lax
from jax.sharding import PartitionSpec as P


def section_terms(adj_tiles, row_slot, live_slot, pieces, totals):
    tile_size = adj_tiles.shape[1]
    piece_rows = pieces[0].shape[0]
    shard_count = piece_rows // tile_size

    def add_tile(k, sums_in):
        tile_now = lax.dynamic_index_in_dim(adj_tiles, k, 0, keepdims=False)
        target = lax.dynamic_index_in_dim(row_slot, k, 0, keepdims=False) * tile_size
        weight_now = lax.dynamic_index_in_dim(live_slot, k, 0, keepdims=False)
        updated = []
        for piece_now, total in zip(pieces, sums_in):
            feat_block = lax.dynamic_slice_in_dim(piece_now, k * tile_size, tile_size, 0)
            tile_term = jnp.dot(tile_now, feat_block, precision=lax.Precision.HIGHEST) * weight_now
            current = lax.dynamic_slice_in_dim(total, target, tile_size, 0)
            updated.append(lax.dynamic_update_slice_in_dim(total, current + tile_term, target, 0))
        return tuple(updated)

    return lax.fori_loop(0, shard_count, add_tile, tuple(totals))


def local(features, weight, bias, adjacency, tile_row, tile_live, node_live, cotangent):
    adj_tiles = adjacency[0, 0]
    row_slot = tile_row[0, 0]
    live_slot = tile_live[0, 0].astype(jnp.float32)
    groups = lax.axis_size("rep")
    tile_size = adj_tiles.shape[1]
    empty_in = jnp.zeros((groups * tile_size, features.shape[1]), jnp.float32)
    partial_in = section_terms(
        adj_tiles,
        row_slot,
        live_slot,
        (lax.all_gather(features, "row", axis=0, tiled=True),),
        (empty_in,),
    )[0]
    aggregated = lax.psum_scatter(partial_in, "rep", scatter_dimension=0, tiled=True)
    projected_sum = jnp.dot(aggregated, weight, precision=lax.Precision.HIGHEST)
    preact = projected_sum + bias
    node_mask = node_live.astype(jnp.float32)[:, None]
    sigmoid_value = jax.nn.sigmoid(preact)
    activations = preact * sigmoid_value * node_mask
    local_grad = cotangent * node_mask * sigmoid_value * (1.0 + preact * (1.0 - sigmoid_value))
    weight_part = lax.dot_general(
        aggregated, local_grad, (((0,), (0,)), ((), ())), precision=lax.Precision.HIGHEST
    )
    bias_part = jnp.sum(local_grad, axis=0)
    weight_grad, bias_grad = lax.psum((weight_part, bias_part), ("row", "rep"))
    return (activations, weight_grad, bias_grad)


def solution(mesh):
    placed = (
        P(("row", "rep"), None),
        P(),
        P(),
        P("row", "rep", None, None, None),
        P("row", "rep", None),
        P("row", "rep", None),
        P(("row", "rep")),
        P(("row", "rep"), None),
    )
    return jax.shard_map(
        local,
        mesh=mesh,
        in_specs=placed,
        out_specs=(P(("row", "rep"), None), P(), P()),
        check_vma=False,
    )
```

profile of v0, /device:TPU:1, one launch (start us, length us, event | category | flops | bytes accessed | tf_op | source)
XLA Modules:
  0.0 943.0 jit_solution(5304687563539046468)
XLA Ops:
  8.6 159.4 %all-gather.2.cloned.1.call-done = f32[8192,128]{1,0:T(8,128)} async-done(((f32[128,128]{1,0:T(8,128)}), f32[8192,128]{1,0:T(8,128)}) %all-gather.2.cloned.1.call-update) | async-done | bytes 4194320 | tf_op jit(solution)/shard_map/all_gather | solution.py:38
  168.1 271.4 %while.13 = (s32[]{:T(128)}, f32[1024,128]{1,0:T(8,128)S(1)}, s32[64]{0:T(128)}, f32[64,128,128]{2,1,0:T(8,128)}, f32[8192,128]{1,0:T(8,128)}, /*index=5*/f32[64...) while((s32[]{:T(128)}, f32[1024,128]{1,0:T(8,128)S(1)}, ...), condition=%wide.region_1.2_spmd, body=%wide.region_0.1_spmd.sunk | while | flops 25198600 | bytes 263409 | solution.py:24
  174.9 1.7 fusion.17
  187.6 1.7 fusion.17
  196.1 1.7 fusion.17
  200.3 1.7 fusion.17
  208.8 1.7 fusion.17
  230.0 1.7 fusion.17
  234.2 1.7 fusion.17
  242.7 1.7 fusion.17
  263.9 1.7 fusion.17
  268.2 1.7 fusion.17
  276.6 1.7 fusion.17
  297.8 1.7 fusion.17
  302.1 1.7 fusion.17
  310.6 1.7 fusion.17
  323.3 1.7 fusion.17
  331.8 1.7 fusion.17
  336.0 1.7 fusion.17
  344.5 1.7 fusion.17
  357.2 1.7 fusion.17
  365.7 1.7 fusion.17
  369.9 1.7 fusion.17
  378.4 1.7 fusion.17
  391.1 1.7 fusion.17
  399.6 1.7 fusion.17
  403.9 1.7 fusion.17
  441.1 34.6 %reduce-scatter.2.cloned.1.call-done = f32[128,128]{1,0:T(8,128)} async-done(((f32[1024,128]{1,0:T(8,128)}), f32[128,128]{1,0:T(8,128)}) %reduce-scatter.2.cloned.1.call-update) | async-done | bytes 65552 | tf_op jit(solution)/shard_map/reduce_scatter | solution.py:41
  475.7 1.9 fusion.6
  477.5 1.8 fusion.7
  479.4 106.9 %psum.15 = f32[256]{0:T(256)} all-reduce(f32[256]{0:T(256)S(1)} %get-tuple-element.125), channel_id=1, replica_groups=mesh['row'=64,'rep'=8] {'row','rep'}, use_global_device_ids=true, to_apply=%region_5.6 | all-reduce | flops 256 | bytes 2048 | tf_op jit(solution)/shard_map/psum | solution.py:52
  586.3 348.6 %all-reduce.2.cloned.1.call-done = f32[128,256]{1,0:T(8,128)} async-done(((f32[128,256]{1,0:T(8,128)}), f32[128,256]{1,0:T(8,128)}) %all-reduce.2.cloned.1.call-update) | async-done | bytes 131088 | tf_op jit(solution)/shard_map/psum | solution.py:52
  (181 shorter events, 188.8 us)
Async XLA Ops:
  7.2 468.5 %copy-start = (f32[128,256]{1,0:T(8,128)S(1)}, f32[128,256]{1,0:T(8,128)}, u32[]{:S(2)}) copy-start(f32[128,256]{1,0:T(8,128)} %param.11) | copy-start | bytes 393220
  7.2 160.9 %all-gather.2.cloned.1.call-start = ((), (), s32[]{:S(2)}) async-start(), calls=%async_computation.1 | async-start | bytes 4259840 | tf_op jit(solution)/shard_map/all_gather | solution.py:38
  7.9 467.7 %reduce-scatter.2.cloned.1.call-start = ((), (), s32[]{:S(2)}) async-start(), calls=%async_computation.2 | async-start | bytes 589824 | tf_op jit(solution)/shard_map/reduce_scatter | solution.py:41
  439.5 0.8 copy-start.1
  440.3 494.6 %all-reduce.2.cloned.1.call-start = ((), (), s32[]{:S(2)}) async-start(), calls=%async_computation.3 | async-start | bytes 262144 | tf_op jit(solution)/shard_map/psum | solution.py:52
Sparse Core Ops, SparseCore 0:
  11.3 156.7 all-gather.1
  440.5 35.1 reduce-scatter.1
  482.6 452.2 all-reduce.1
where the time goes:
time: 948 us; the launch traced here: 943 us
  waiting for transfers between devices  543 us (57%)
  local copies, waits for them, and re-layouts  119 us (13%)
  matrix products  114 us (12%)
  blocking collectives  107 us (11%)
  loops' own time  44.1 us (5%)
  between operations  13.8 us (1%)
    psum x1, waiting for transfers between devices, local(): weight_grad, bias_grad = lax.psum((weight_part, bias_part), ('row', 'rep'))  349 us
    all_gather x1, waiting for transfers between devices, local(): lax.all_gather(features, 'row', axis=0, tiled=True)  159 us
    dot_general x64, matrix products, add_tile(): jnp.dot(tile_now, feat_block, precision=lax.Precision.HIGHEST) * weight_now  110 us
    psum x1, blocking collectives, local(): weight_grad, bias_grad = lax.psum((weight_part, bias_part), ('row', 'rep'))  107 us
    dynamic_slice x64, local copies, waits for them, and re-layouts, add_tile(): lax.dynamic_index_in_dim(row_slot, k, 0, keepdims=False) * tile_size  79.5 us
    another operation x1, loops' own time, section_terms(): return lax.fori_loop(0, shard_count, add_tile, tuple(totals))  44.1 us
    dynamic_slice x64, local copies, waits for them, and re-layouts, add_tile(): weight_now = lax.dynamic_index_in_dim(live_slot, k, 0, keepdims=False)  37.5 us
    reduce_scatter x1, waiting for transfers between devices, local(): lax.psum_scatter(partial_in, 'rep', scatter_dimension=0, tiled=True)  34.6 us
  transfers between devices with their start and end apart: 3, of which 3 were waited for; matrix products, arithmetic and copies ran while one was open for 0% of the time, Pallas kernels for 0%

commit v1 on v0

v1 whole, which is shorter than its diff:
```python
import functools

import jax
import jax.numpy as jnp
from jax import lax
from jax.experimental import pallas as pl
from jax.experimental.pallas import tpu as pltpu
from jax.sharding import PartitionSpec as P

MESH = pl.DeviceIdType.MESH
F32 = jnp.float32
BF16 = jnp.bfloat16


def split(x):
    high = x.astype(BF16)
    return high, (x - high.astype(F32)).astype(BF16)


def arrived(ref, sem):
    pltpu.make_async_copy(ref, ref, sem).wait()


def kernel(
    feat,
    weight,
    bias,
    adj,
    trow,
    tlive,
    nlive,
    cot,
    act_out,
    wg_out,
    bg_out,
    gathered,
    tiles,
    wv,
    cv,
    acc,
    prods,
    incoming,
    av,
    part,
    plane_in,
    reduced,
    z_in,
    final,
    wsum,
    bpart,
    bplane,
    breduced,
    bz,
    bfinal,
    bsum,
    lsem,
    tsem,
    ssem,
    rsem,
    xs,
    xr,
    as_,
    ar,
    bs,
    br,
    osem,
):
    row = lax.axis_index("row")
    rep = lax.axis_index("rep")
    nz = lax.axis_size("row") // 4
    nrep = lax.axis_size("rep")
    nplane = 4 * nrep
    z, h, k = row // 4, (row // 2) % 2, row % 2
    d = 1 - 2 * k
    half = nz // 2

    def slab(t):
        return (z + t * d + nz) % nz

    def block(zz, hh, kk):
        return zz * 4 + hh * 2 + kk

    def at_device(r, p):
        return {"row": r, "rep": p}

    partner = at_device(block(z, h, 1 - k), rep)
    ahead = at_device(block(slab(1), h, k), rep)
    behind = at_device(block(slab(-1), h, k), rep)
    across = at_device(block(z, 1 - h, k), rep)

    barrier = pltpu.get_barrier_semaphore()

    def greet(dev):
        pl.semaphore_signal(barrier, inc=1, device_id=dev, device_id_type=MESH)

    greet(behind)
    greet(partner)
    greet(across)
    for j in range(1, nrep):
        greet(at_device(row, (rep + j) % nrep))

    tile_copy = pltpu.make_async_copy(adj, tiles, tsem)
    tile_copy.start()
    own_copy = pltpu.make_async_copy(feat, gathered.at[row], lsem.at[0])
    own_copy.start()
    w_copy = pltpu.make_async_copy(weight, wv, lsem.at[1])
    w_copy.start()
    c_copy = pltpu.make_async_copy(cot, cv, lsem.at[2])
    c_copy.start()
    pl.semaphore_wait(barrier, 3 + nrep - 1)

    def send(src, slot, dev):
        pltpu.make_async_remote_copy(
            src_ref=src,
            dst_ref=gathered.at[slot],
            send_sem=ssem,
            recv_sem=rsem.at[slot],
            device_id=dev,
            device_id_type=MESH,
        ).start()

    def take(slot):
        arrived(gathered.at[slot], rsem.at[slot])

    def group(zz):
        for j in range(4):
            s = zz * 4 + j
            fh, fl = split(gathered[s])
            right = jnp.concatenate([fh, fl], axis=1)
            right = jnp.concatenate([right, right], axis=0)
            ah, al = split(tiles[s])
            left = jnp.concatenate([ah, al], axis=1)
            both = jnp.dot(left, right, preferred_element_type=F32)
            prods[j] = both[:, :128] + both[:, 128:]
        picks = []
        for j in range(4):
            s = zz * 4 + j
            live = tlive[0, s].astype(F32)
            picks.append([jnp.where(trow[0, s] == a, live, 0.0) for a in range(8)])
        for a in range(8):
            total = acc[a]
            for j in range(4):
                total = total + prods[j] * picks[j][a]
            acc[a] = total

    send(feat, row, ahead)
    send(feat, row, partner)
    send(feat, row, across)
    acc[...] = jnp.zeros_like(acc)
    first = block(z, h, 1 - k)
    take(first)
    send(gathered.at[first], first, ahead)
    second = block(z, 1 - h, k)
    take(second)
    send(gathered.at[second], second, ahead)
    send(gathered.at[second], second, partner)
    third = block(z, 1 - h, 1 - k)
    take(third)
    send(gathered.at[third], third, ahead)

    def pass_on(t):
        zz = slab(-t)
        for at, (hh, kk) in enumerate(((h, k), (h, 1 - k), (1 - h, k), (1 - h, 1 - k))):
            slot = block(zz, hh, kk)
            take(slot)
            if at % 2 == 0:
                send(gathered.at[slot], slot, ahead)
            else:

                @pl.when(t < half - 1)
                def _():
                    send(gathered.at[slot], slot, ahead)

            send(gathered.at[slot], slot, partner)

    def take_slab(zz):
        for j in range(4):
            take(zz * 4 + j)

    pass_on(1)
    tile_copy.wait()
    own_copy.wait()
    group(z)

    def step(t, carry):
        pass_on(t)
        group(slab(1 - t))
        take_slab(slab(t - 1))
        group(slab(t - 1))
        return carry

    lax.fori_loop(2, half, step, 0)
    far = slab(half)
    for hh in (h, 1 - h):
        slot = block(far, hh, k)
        take(slot)
        send(gathered.at[slot], slot, partner)
    group(slab(1 - half))
    take_slab(slab(half - 1))
    group(slab(half - 1))
    for hh in (h, 1 - h):
        take(block(far, hh, 1 - k))
    group(far)

    for j in range(1, nrep):
        to = (rep + j) % nrep
        pltpu.make_async_remote_copy(
            src_ref=acc.at[to],
            dst_ref=incoming.at[j],
            send_sem=xs,
            recv_sem=xr,
            device_id=at_device(row, to),
            device_id_type=MESH,
        ).start()
    w_copy.wait()
    c_copy.wait()
    wh, wl = split(wv[...])
    live = jnp.transpose(jnp.broadcast_to(nlive[...].astype(F32), (128, 128)))
    mask = jnp.concatenate([live, live], axis=1)
    arrived(incoming.at[pl.ds(1, nrep - 1)], xr)
    agg = acc[rep]
    for j in range(1, nrep):
        agg = agg + incoming[j]
    ah, al = split(agg)
    pre = jnp.dot(
        jnp.concatenate([ah, al], axis=1),
        jnp.concatenate([wh, wh], axis=0),
        preferred_element_type=F32,
    )
    pre = pre + jnp.dot(ah, wl, preferred_element_type=F32) + bias[...]
    sig = jax.nn.sigmoid(pre)
    av[...] = pre * sig * mask
    act_copy = pltpu.make_async_copy(av, act_out, osem.at[0])
    act_copy.start()
    grad = cv[...] * mask * sig * (1.0 + pre * (1.0 - sig))
    gh, gl = split(grad)
    along = (((0,), (0,)), ((), ()))
    wpart = lax.dot_general(
        jnp.concatenate([ah, al], axis=0),
        jnp.concatenate([gh, gh], axis=0),
        along,
        preferred_element_type=F32,
    ) + lax.dot_general(ah, gl, along, preferred_element_type=F32)
    part[pl.ds(0, 16)] = wpart[:, :128].reshape(16, 8, 128)
    part[pl.ds(16, 16)] = wpart[:, 128:].reshape(16, 8, 128)
    bias_sum = jnp.sum(grad, axis=0, keepdims=True)
    bpart[...] = jnp.zeros_like(bpart)
    bpart[0:1] = bias_sum[:, :128]
    bpart[1:2] = bias_sum[:, 128:]

    me = (row % 4) * nrep + rep

    def plane_device(q):
        return at_device(z * 4 + q // nrep, q % nrep)

    def copy_to(src, dst, at, dev):
        pltpu.make_async_remote_copy(
            src_ref=src,
            dst_ref=dst,
            send_sem=as_.at[at],
            recv_sem=ar.at[at],
            device_id=dev,
            device_id_type=MESH,
        ).start()

    def bcopy(src, dst, at, dev):
        return pltpu.make_async_remote_copy(
            src_ref=src,
            dst_ref=dst,
            send_sem=bs.at[at],
            recv_sem=br.at[at],
            device_id=dev,
            device_id_type=MESH,
        )

    def scatter(j, carry):
        q = (me + j) % nplane
        copy_to(part.at[q], plane_in.at[j], 0, plane_device(q))
        return carry

    lax.fori_loop(1, nplane, scatter, 0)

    @pl.when(me != 0)
    def _():
        bcopy(bpart, bplane.at[me], 0, plane_device(0)).start()

    arrived(plane_in.at[pl.ds(1, nplane - 1)], ar.at[0])
    total = part[me]
    for j in range(1, nplane):
        total = total + plane_in[j]
    reduced[...] = total
    z_in[z] = total

    def along_z(j, carry):
        zz = (z + j) % nz
        copy_to(reduced, z_in.at[z], 1, at_device(zz * 4 + row % 4, rep))
        return carry

    lax.fori_loop(1, nz, along_z, 0)

    @pl.when(me == 0)
    def _():
        arrived(bplane.at[pl.ds(1, nplane - 1)], br.at[0])
        btotal = bpart[...]
        for j in range(1, nplane):
            btotal = btotal + bplane[j]
        breduced[...] = btotal
        bz[z] = btotal

        def balong(j, carry):
            zz = (z + j) % nz
            bcopy(breduced, bz.at[z], 1, at_device(zz * 4 + row % 4, rep)).start()
            return carry

        lax.fori_loop(1, nz, balong, 0)

    arrived(z_in.at[pl.ds(1, nz - 1)], ar.at[1])
    total = z_in[0]
    for j in range(1, nz):
        total = total + z_in[j]
    final[...] = total
    wsum[me] = total

    def gather(j, carry):
        q = (me + j) % nplane
        copy_to(final, wsum.at[me], 2, plane_device(q))
        return carry

    lax.fori_loop(1, nplane, gather, 0)

    @pl.when(me == 0)
    def _():
        arrived(bz.at[pl.ds(1, nz - 1)], br.at[1])
        btotal = bz[0]
        for j in range(1, nz):
            btotal = btotal + bz[j]
        bfinal[...] = btotal
        bsum[...] = btotal

        def bgather(j, carry):
            bcopy(bfinal, bsum, 2, plane_device(j)).start()
            return carry

        lax.fori_loop(1, nplane, bgather, 0)

    arrived(wsum.at[pl.ds(1, nplane - 1)], ar.at[2])
    wg_out[:, :128] = wsum[pl.ds(0, 16)].reshape(128, 128)
    wg_out[:, 128:] = wsum[pl.ds(16, 16)].reshape(128, 128)

    @pl.when(me != 0)
    def _():
        arrived(bsum, br.at[2])
        arrived(bpart, bs.at[0])

    bg_out[:, :128] = bsum[0:1]
    bg_out[:, 128:] = bsum[1:2]

    @pl.when(me == 0)
    def _():
        arrived(bz.at[pl.ds(1, nz - 1)], bs.at[1])
        arrived(bplane.at[pl.ds(1, nplane - 1)], bs.at[2])

    sent = nz * 4 - 1
    arrived(gathered.at[pl.ds(0, sent)], ssem)
    arrived(incoming.at[pl.ds(1, nrep - 1)], xs)
    arrived(plane_in.at[pl.ds(1, nplane - 1)], as_.at[0])
    arrived(z_in.at[pl.ds(1, nz - 1)], as_.at[1])
    arrived(plane_in.at[pl.ds(1, nplane - 1)], as_.at[2])
    act_copy.wait()


def local(features, weight, bias, adjacency, tile_row, tile_live, node_live, cotangent):
    count = adjacency.shape[2]
    nrep = lax.axis_size("rep")
    nplane = 4 * nrep
    nz = lax.axis_size("row") // 4
    hbm = pl.BlockSpec(memory_space=pltpu.HBM)
    vmem = pl.BlockSpec(memory_space=pltpu.VMEM)
    smem = pl.BlockSpec(memory_space=pltpu.SMEM)
    dma = pltpu.SemaphoreType.DMA
    act, wg, bg = pl.pallas_call(
        kernel,
        out_shape=(
            jax.ShapeDtypeStruct((128, 256), F32),
            jax.ShapeDtypeStruct((128, 256), F32),
            jax.ShapeDtypeStruct((1, 256), F32),
        ),
        in_specs=[hbm, hbm, vmem, hbm, smem, smem, vmem, hbm],
        out_specs=(hbm, vmem, vmem),
        scratch_shapes=[
            pltpu.VMEM((count, 128, 128), F32),
            pltpu.VMEM((count, 128, 128), F32),
            pltpu.VMEM((128, 256), F32),
            pltpu.VMEM((128, 256), F32),
            pltpu.VMEM((nrep, 128, 128), F32),
            pltpu.VMEM((4, 128, 128), F32),
            pltpu.VMEM((nrep, 128, 128), F32),
            pltpu.VMEM((128, 256), F32),
            pltpu.VMEM((nplane, 8, 128), F32),
            pltpu.VMEM((nplane, 8, 128), F32),
            pltpu.VMEM((8, 128), F32),
            pltpu.VMEM((nz, 8, 128), F32),
            pltpu.VMEM((8, 128), F32),
            pltpu.VMEM((nplane, 8, 128), F32),
            pltpu.VMEM((8, 128), F32),
            pltpu.VMEM((nplane, 8, 128), F32),
            pltpu.VMEM((8, 128), F32),
            pltpu.VMEM((nz, 8, 128), F32),
            pltpu.VMEM((8, 128), F32),
            pltpu.VMEM((8, 128), F32),
            dma((3,)),
            dma,
            dma,
            dma((count,)),
            dma,
            dma,
            dma((3,)),
            dma((3,)),
            dma((3,)),
            dma((3,)),
            dma((1,)),
        ],
        compiler_params=pltpu.CompilerParams(
            collective_id=0, has_side_effects=True, vmem_limit_bytes=48 * 1024 * 1024
        ),
    )(
        features,
        weight,
        bias.reshape(1, 256),
        adjacency.reshape(count, 128, 128),
        tile_row.reshape(1, count),
        tile_live.reshape(1, count),
        node_live.reshape(1, 128),
        cotangent,
    )
    return act, wg, bg.reshape(256)


def solution(mesh):
    placed = (
        P(("row", "rep"), None),
        P(),
        P(),
        P("row", "rep", None, None, None),
        P("row", "rep", None),
        P("row", "rep", None),
        P(("row", "rep")),
        P(("row", "rep"), None),
    )
    return jax.shard_map(
        local,
        mesh=mesh,
        in_specs=placed,
        out_specs=(P(("row", "rep"), None), P(), P()),
        check_vma=False,
    )
```

time: 948 us -> 84.7 us (0.09)
  waiting for transfers between devices: 543 us -> 0 us
  matrix products: 114 us -> 0 us
  local copies, waits for them, and re-layouts: 119 us -> 9.35 us
  blocking collectives: 107 us -> 0 us
  Pallas kernels: 0 us -> 74.4 us
  loops' own time: 44.1 us -> 0 us
  between operations: 13.8 us -> 0.66 us
    psum x1 -> x0, waiting for transfers between devices: 349 us -> none  [local(): weight_grad, bias_grad = lax.psum((weight_part, bias_part), ('row', 'rep'))]
    all_gather x1 -> x0, waiting for transfers between devices: 159 us -> none  [local(): lax.all_gather(features, 'row', axis=0, tiled=True)]
    dynamic_slice x128 -> x0, local copies, waits for them, and re-layouts: 117 us -> none  [the longest x64 79.5 us: add_tile(): lax.dynamic_index_in_dim(row_slot, k, 0, keepdims=False) * tile_size]
    dot_general x66 -> x0, matrix products: 114 us -> none  [the longest x64 110 us: add_tile(): jnp.dot(tile_now, feat_block, precision=lax.Precision.HIGHEST) * weight_now]
    psum x1 -> x0, blocking collectives: 107 us -> none  [local(): weight_grad, bias_grad = lax.psum((weight_part, bias_part), ('row', 'rep'))]
    pallas_call x0 -> x1, Pallas kernels: none -> 74.4 us  [local(): pl.pallas_call(kernel, out_shape=(jax.ShapeDtypeStruct((128, 256), F32),...]
    another operation x1 -> x0, loops' own time: 44.1 us -> none  [section_terms(): return lax.fori_loop(0, shard_count, add_tile, tuple(totals))]
    reduce_scatter x1 -> x0, waiting for transfers between devices: 34.6 us -> none  [local(): lax.psum_scatter(partial_in, 'rep', scatter_dimension=0, tiled=True)]
  transfers between devices with their start and end apart: 3 -> 0, of which waited for: 3 -> 0; matrix products, arithmetic and copies ran while one was open for 0% -> 0% of each run, Pallas kernels for 0% -> 0%
where the time goes in v1:
time: 84.7 us; the launch traced here: 84.4 us
  Pallas kernels  74.4 us (88%)
  local copies, waits for them, and re-layouts  9.35 us (11%)
    pallas_call x1, Pallas kernels, local(): pl.pallas_call(kernel, out_shape=(jax.ShapeDtypeStruct((128, 256), F32),...  74.4 us
    unnamed x19, local copies, waits for them, and re-layouts  9.35 us

profile of v1, /device:TPU:1, one launch (start us, length us, event | category | flops | bytes accessed | tf_op | source)
XLA Modules:
  0.0 84.4 jit_solution(13919664177437142807)
XLA Ops:
  0.6 0.0 copy-start
  0.6 2.2 %copy-done = f32[1,1,64,128,128]{4,3,2,1,0:T(8,128)S(1)} copy-done((f32[1,1,64,128,128]{4,3,2,1,0:T(8,128)S(1)}, f32[1,1,64,128,128]{4,3,2,1,0:T(8,128)}, u32[]{:S(2)}) %copy-start) | copy-done | bytes 4194328
  2.8 0.0 copy-start.1
  2.8 0.9 %copy-done.1 = f32[128,256]{1,0:T(8,128)S(1)} copy-done((f32[128,256]{1,0:T(8,128)S(1)}, f32[128,256]{1,0:T(8,128)}, u32[]{:S(2)}) %copy-start.1) | copy-done | bytes 131096
  3.7 0.0 copy-start.2
  3.7 0.9 %copy-done.2 = f32[128,256]{1,0:T(8,128)S(1)} copy-done((f32[128,256]{1,0:T(8,128)S(1)}, f32[128,256]{1,0:T(8,128)}, u32[]{:S(2)}) %copy-start.2) | copy-done | bytes 131096
  4.6 0.0 copy-start.3
  4.6 0.8 copy-done.3
  5.5 0.0 copy-start.4
  5.5 0.7 copy-done.4
  6.2 0.0 copy-start.5
  6.2 0.7 copy-done.5
  6.8 0.0 copy-start.6
  6.8 0.7 copy-done.6
  7.5 0.0 copy-start.7
  7.5 0.7 copy-done.7
  8.1 74.4 %shard_map.103 = (f32[128,256]{1,0:T(8,128)S(1)}, f32[128,256]{1,0:T(8,128)S(1)}, f32[1,256]{1,0:T(1,128)S(1)}) custom-call(f32[128,128]{1,0:T(8,128)S(1)} %copy-done.3, f32[128,256]{1,0:T(8,128)S(1)} %copy-done.1, f32[1,256]{1,0:T(1,128)S(1)} %bitcast.7, f32[64,128,128]{2,1,0:T(8,128)S(1)} %bitcast.6, s32[1,64]{1,0:T(1,128)S(1)} %bitcast.9, ...), custom_call_target="tpu_custom_call" | custom-call | tf_op jit(solution)/shard_map/pallas_call | solution.py:381
  82.5 0.7 copy.14
  83.2 0.7 copy.15
  83.8 0.6 copy.16
Async XLA Ops:
  0.6 2.2 %copy-start = (f32[1,1,64,128,128]{4,3,2,1,0:T(8,128)S(1)}, f32[1,1,64,128,128]{4,3,2,1,0:T(8,128)}, u32[]{:S(2)}) copy-start(f32[1,1,64,128,128]{4,3,2,1,0:T(8,128)} %param.11) | copy-start | bytes 12582916
  2.8 0.9 %copy-start.1 = (f32[128,256]{1,0:T(8,128)S(1)}, f32[128,256]{1,0:T(8,128)}, u32[]{:S(2)}) copy-start(f32[128,256]{1,0:T(8,128)} %weight.1) | copy-start | bytes 393220
  3.7 0.9 %copy-start.2 = (f32[128,256]{1,0:T(8,128)S(1)}, f32[128,256]{1,0:T(8,128)}, u32[]{:S(2)}) copy-start(f32[128,256]{1,0:T(8,128)} %cot.1) | copy-start | bytes 393220
  4.6 0.8 copy-start.3
  5.5 0.7 copy-start.4
  6.2 0.7 copy-start.5
  6.8 0.7 copy-start.6
  7.5 0.7 copy-start.7

commit v2 on v1

v2 whole, which is shorter than its diff:
```python
import functools

import jax
import jax.numpy as jnp
from jax import lax
from jax.experimental import pallas as pl
from jax.experimental.pallas import tpu as pltpu
from jax.sharding import PartitionSpec as P

MESH = pl.DeviceIdType.MESH
F32 = jnp.float32
CHUNKS = 1
PLANE = sorted(
    ((dx, dy, dk) for dx in range(4) for dy in range(4) for dk in range(2)),
    key=lambda d: -(min(d[0], 4 - d[0]) + min(d[1], 4 - d[1])) * 2 - d[2],
)[:-1]
BF16 = jnp.bfloat16


def split(x):
    high = x.astype(BF16)
    return high, (x - high.astype(F32)).astype(BF16)


def arrived(ref, sem):
    pltpu.make_async_copy(ref, ref, sem).wait()


def kernel(
    feat,
    weight,
    bias,
    adj,
    trow,
    tlive,
    nlive,
    cot,
    act_out,
    wg_out,
    bg_out,
    gathered,
    tiles,
    wv,
    cv,
    acc,
    prods,
    incoming,
    av,
    part,
    plane_in,
    reduced,
    z_in,
    final,
    wsum,
    bpart,
    bplane,
    breduced,
    bz,
    bfinal,
    bsum,
    row_s,
    live_s,
    bias_v,
    node_v,
    ready,
    lsem,
    tsem,
    ssem,
    rsem,
    xs,
    xr,
    as_,
    ar,
    bs,
    br,
    osem,
):
    row = lax.axis_index("row")
    rep = lax.axis_index("rep")
    nz = lax.axis_size("row") // 4
    nrep = lax.axis_size("rep")
    nplane = 4 * nrep
    rows = 128 // CHUNKS
    z, h, k = row // 4, (row // 2) % 2, row % 2
    d = 1 - 2 * k

    def slab(t):
        return (z + t * d + nz) % nz

    def block(zz, hh, kk):
        return zz * 4 + hh * 2 + kk

    def at_device(r, p):
        return {"row": r, "rep": p}

    partner = at_device(block(z, h, 1 - k), rep)
    ahead = {t: at_device(block(slab(t), h, k), rep) for t in (1, 2)}
    across = at_device(block(z, 1 - h, k), rep)

    barrier = pltpu.get_barrier_semaphore()

    def greet(dev):
        pl.semaphore_signal(barrier, inc=1, device_id=dev, device_id_type=MESH)

    for t in (1, 2):
        greet(at_device(block(slab(-t), h, k), rep))
    greet(partner)
    greet(across)
    y, side_x = rep // 2, rep % 2
    ny = nrep // 2
    beside = [at_device(row, ((y + dy) % ny) * 2 + side_x) for dy in (1, 3)]
    for dev in beside:
        greet(dev)
    greet(at_device(row, y * 2 + 1 - side_x))

    own_copy = pltpu.make_async_copy(feat, gathered.at[row], lsem.at[0])
    own_copy.start()
    row_copy = pltpu.make_async_copy(trow, row_s, lsem.at[3])
    row_copy.start()
    live_copy = pltpu.make_async_copy(tlive, live_s, lsem.at[4])
    live_copy.start()
    tile_copy = pltpu.make_async_copy(adj, tiles, tsem)
    tile_copy.start()
    w_copy = pltpu.make_async_copy(weight, wv, lsem.at[1])
    w_copy.start()
    c_copy = pltpu.make_async_copy(cot, cv, lsem.at[2])
    c_copy.start()
    bias_copy = pltpu.make_async_copy(bias, bias_v, lsem.at[5])
    bias_copy.start()
    node_copy = pltpu.make_async_copy(nlive, node_v, lsem.at[6])
    node_copy.start()
    pl.semaphore_wait(barrier, 7)

    def tell(at):
        for dev in beside:
            pl.semaphore_signal(ready.at[at], inc=1, device_id=dev, device_id_type=MESH)

    own_copy.wait()

    def piece(slot, c):
        return gathered.at[slot, pl.ds(c * rows, rows)]

    def push(src, slot, c, dev):
        pltpu.make_async_remote_copy(
            src_ref=src,
            dst_ref=piece(slot, c),
            send_sem=ssem,
            recv_sem=rsem.at[slot, c],
            device_id=dev,
            device_id_type=MESH,
        ).start()

    def first(c, dev):
        push(piece(row, c), row, c, dev)

    def send(slot, c, dev):
        push(piece(slot, c), slot, c, dev)

    def take(slot, c):
        arrived(piece(slot, c), rsem.at[slot, c])

    def take_all(slot):
        for c in range(CHUNKS):
            take(slot, c)

    def pair(zz, hh):
        base = zz * 4 + hh * 2
        for j in range(2):
            fh, fl = split(gathered[base + j])
            right = jnp.concatenate([fh, fl], axis=1)
            right = jnp.concatenate([right, right], axis=0)
            ah, al = split(tiles[base + j])
            left = jnp.concatenate([ah, al], axis=1)
            both = jnp.dot(left, right, preferred_element_type=F32)
            prods[j] = both[:, :128] + both[:, 128:]
        picks = []
        for j in range(2):
            live = live_s[0, base + j].astype(F32)
            target = row_s[0, base + j]
            picks.append([jnp.where(target == a, live, 0.0) for a in range(8)])
        for a in range(8):
            acc[a] = acc[a] + (prods[0] * picks[0][a] + prods[1] * picks[1][a])

    def duo(t, hh):
        for kk in range(2):
            take_all(block(slab(t), hh, kk))

        def side(i, carry):
            pair(slab(t * (2 * i - 1)), hh)
            return carry

        lax.fori_loop(0, 2, side, 0)

    other = 1 - k

    def ring(t):
        for c in range(CHUNKS):
            for kk, end in ((k, 8), (other, 7)):
                if t > end:
                    continue
                slot = block(slab(-t), h, kk)
                take(slot, c)
                if t % 2 == 0:
                    for hop in (2, 1):
                        if t + hop <= end:
                            send(slot, c, ahead[hop])
                send(slot, c, across)
                send(slot, c, partner)

    def crossed(t):
        for c in range(CHUNKS):
            for kk, end in ((k, 8), (other, 7)):
                if t > end or (t == 0 and kk is other):
                    continue
                slot = block(slab(-t), 1 - h, kk)
                take(slot, c)
                send(slot, c, partner)

    for c in range(CHUNKS):
        first(c, partner)
        for hop in (2, 1):
            first(c, ahead[hop])
        first(c, across)
    tell(0)
    acc[...] = jnp.zeros_like(acc)
    mine = block(z, h, other)
    for c in range(CHUNKS):
        take(mine, c)
        for hop in (2, 1):
            send(mine, c, ahead[hop])
    tile_copy.wait()
    row_copy.wait()
    live_copy.wait()
    ring(2)
    pl.semaphore_wait(ready.at[0], 2)
    tell(1)
    pair(z, h)
    ring(1)
    duo(2, h)
    for t in (4, 6):
        ring(t)
        duo(t - 3, h)
        ring(t - 1)
        duo(t, h)
    ring(8)
    ring(7)
    for t in (0, 2, 1, 4, 3):
        crossed(t)
    duo(5, h)
    take_all(block(z, 1 - h, other))
    pair(z, 1 - h)
    duo(2, 1 - h)
    duo(1, 1 - h)
    for t in (6, 5):
        crossed(t)
    duo(7, h)
    take_all(block(slab(8), h, other))
    pair(slab(8), h)
    duo(4, 1 - h)
    crossed(8)
    crossed(7)
    for t in (3, 6, 5, 7):
        duo(t, 1 - h)
    take_all(block(slab(8), 1 - h, other))
    pair(slab(8), 1 - h)

    pl.semaphore_wait(ready.at[1], 2)
    for dy, dx in ((2, 1), (1, 1), (3, 1), (0, 1), (2, 0), (1, 0), (3, 0)):
        to = ((y + dy) % ny) * 2 + (side_x + dx) % 2
        pltpu.make_async_remote_copy(
            src_ref=acc.at[to],
            dst_ref=incoming.at[dy * 2 + dx],
            send_sem=xs,
            recv_sem=xr,
            device_id=at_device(row, to),
            device_id_type=MESH,
        ).start()
    w_copy.wait()
    c_copy.wait()
    bias_copy.wait()
    node_copy.wait()
    wh, wl = split(wv[...])
    live = jnp.transpose(jnp.broadcast_to(node_v[...].astype(F32), (128, 128)))
    mask = jnp.concatenate([live, live], axis=1)
    arrived(incoming.at[pl.ds(1, nrep - 1)], xr)
    agg = acc[rep]
    for j in range(1, nrep):
        agg = agg + incoming[j]
    ah, al = split(agg)
    pre = jnp.dot(
        jnp.concatenate([ah, al], axis=1),
        jnp.concatenate([wh, wh], axis=0),
        preferred_element_type=F32,
    )
    pre = pre + jnp.dot(ah, wl, preferred_element_type=F32) + bias_v[...]
    sig = jax.nn.sigmoid(pre)
    av[...] = pre * sig * mask
    act_copy = pltpu.make_async_copy(av, act_out, osem.at[0])
    act_copy.start()
    grad = cv[...] * mask * sig * (1.0 + pre * (1.0 - sig))
    gh, gl = split(grad)
    along = (((0,), (0,)), ((), ()))
    wpart = lax.dot_general(
        jnp.concatenate([ah, al], axis=0),
        jnp.concatenate([gh, gh], axis=0),
        along,
        preferred_element_type=F32,
    ) + lax.dot_general(ah, gl, along, preferred_element_type=F32)
    part[pl.ds(0, 16)] = wpart[:, :128].reshape(16, 8, 128)
    part[pl.ds(16, 16)] = wpart[:, 128:].reshape(16, 8, 128)
    bias_sum = jnp.sum(grad, axis=0, keepdims=True)
    bpart[...] = jnp.zeros_like(bpart)
    bpart[0:1] = bias_sum[:, :128]
    bpart[1:2] = bias_sum[:, 128:]

    me = (row % 4) * nrep + rep

    x = h * 2 + side_x
    xs_at = [(x + dx) % 4 for dx in range(4)]
    row_at = [[z * 4 + xx // 2 * 2 + (k + dk) % 2 for dk in range(2)] for xx in xs_at]
    rep_at = [[(y + dy) % ny * 2 + xx % 2 for dy in range(4)] for xx in xs_at]

    def plane_peers():
        for j, (dx, dy, dk) in enumerate(PLANE):
            r, p = row_at[dx][dk], rep_at[dx][dy]
            yield j + 1, (r - z * 4) * nrep + p, at_device(r, p)

    z_far = sorted(range(1, nz), key=lambda j: -min(j, nz - j))

    def z_peers():
        for j in z_far:
            yield at_device((z + j) % nz * 4 + row % 4, rep)

    def copy_to(src, dst, at, dev):
        pltpu.make_async_remote_copy(
            src_ref=src,
            dst_ref=dst,
            send_sem=as_.at[at],
            recv_sem=ar.at[at],
            device_id=dev,
            device_id_type=MESH,
        ).start()

    def bcopy(src, dst, at, dev):
        return pltpu.make_async_remote_copy(
            src_ref=src,
            dst_ref=dst,
            send_sem=bs.at[at],
            recv_sem=br.at[at],
            device_id=dev,
            device_id_type=MESH,
        )

    for j, q, dev in plane_peers():
        copy_to(part.at[q], plane_in.at[j], 0, dev)

    @pl.when(me != 0)
    def _():
        bcopy(bpart, bplane.at[me], 0, at_device(z * 4, 0)).start()

    arrived(plane_in.at[pl.ds(1, nplane - 1)], ar.at[0])
    total = part[me]
    for j in range(1, nplane):
        total = total + plane_in[j]
    reduced[...] = total
    z_in[z] = total

    for dev in z_peers():
        copy_to(reduced, z_in.at[z], 1, dev)

    @pl.when(me == 0)
    def _():
        arrived(bplane.at[pl.ds(1, nplane - 1)], br.at[0])
        btotal = bpart[...]
        for j in range(1, nplane):
            btotal = btotal + bplane[j]
        breduced[...] = btotal
        bz[z] = btotal

        def balong(j, carry):
            zz = (z + j) % nz
            bcopy(breduced, bz.at[z], 1, at_device(zz * 4 + row % 4, rep)).start()
            return carry

        lax.fori_loop(1, nz, balong, 0)

    arrived(z_in.at[pl.ds(1, nz - 1)], ar.at[1])
    total = z_in[0]
    for j in range(1, nz):
        total = total + z_in[j]
    final[...] = total
    wsum[me] = total

    for j, q, dev in plane_peers():
        copy_to(final, wsum.at[me], 2, dev)

    @pl.when(me == 0)
    def _():
        arrived(bz.at[pl.ds(1, nz - 1)], br.at[1])
        btotal = bz[0]
        for j in range(1, nz):
            btotal = btotal + bz[j]
        bfinal[...] = btotal
        bsum[...] = btotal

        def bgather(j, carry):
            bcopy(bfinal, bsum, 2, at_device(z * 4 + j // nrep, j % nrep)).start()
            return carry

        lax.fori_loop(1, nplane, bgather, 0)

    arrived(wsum.at[pl.ds(1, nplane - 1)], ar.at[2])
    wg_out[:, :128] = wsum[pl.ds(0, 16)].reshape(128, 128)
    wg_out[:, 128:] = wsum[pl.ds(16, 16)].reshape(128, 128)

    @pl.when(me != 0)
    def _():
        arrived(bsum, br.at[2])
        arrived(bpart, bs.at[0])

    bg_out[:, :128] = bsum[0:1]
    bg_out[:, 128:] = bsum[1:2]

    @pl.when(me == 0)
    def _():
        arrived(bz.at[pl.ds(1, nz - 1)], bs.at[1])
        arrived(bplane.at[pl.ds(1, nplane - 1)], bs.at[2])

    sent = nz * 4 - 1
    arrived(gathered.at[pl.ds(0, sent)], ssem)
    arrived(incoming.at[pl.ds(1, nrep - 1)], xs)
    arrived(plane_in.at[pl.ds(1, nplane - 1)], as_.at[0])
    arrived(z_in.at[pl.ds(1, nz - 1)], as_.at[1])
    arrived(plane_in.at[pl.ds(1, nplane - 1)], as_.at[2])
    act_copy.wait()


def writer(act, wg, bg, act_out, wg_out, bg_out, sems):
    copies = [
        pltpu.make_async_copy(src, dst, sems.at[i])
        for i, (src, dst) in enumerate(((act, act_out), (wg, wg_out), (bg, bg_out)))
    ]
    for copy in copies:
        copy.start()
    for copy in copies:
        copy.wait()


def write_out(act, wg, bg):
    vmem = pl.BlockSpec(memory_space=pltpu.VMEM)
    hbm = pl.BlockSpec(memory_space=pltpu.HBM)
    act, wg, bg = pl.pallas_call(
        writer,
        out_shape=tuple(jax.ShapeDtypeStruct(x.shape, F32) for x in (act, wg, bg)),
        in_specs=[vmem] * 3,
        out_specs=(hbm,) * 3,
        scratch_shapes=[pltpu.SemaphoreType.DMA((3,))],
        compiler_params=pltpu.CompilerParams(vmem_limit_bytes=4 * 1024 * 1024),
    )(act, wg, bg)
    return act, wg, bg.reshape(256)


def local(features, weight, bias, adjacency, tile_row, tile_live, node_live, cotangent):
    count = adjacency.shape[2]
    nrep = lax.axis_size("rep")
    nplane = 4 * nrep
    nz = lax.axis_size("row") // 4
    hbm = pl.BlockSpec(memory_space=pltpu.HBM)
    vmem = pl.BlockSpec(memory_space=pltpu.VMEM)
    dma = pltpu.SemaphoreType.DMA
    act, wg, bg = pl.pallas_call(
        kernel,
        out_shape=(
            jax.ShapeDtypeStruct((128, 256), F32),
            jax.ShapeDtypeStruct((128, 256), F32),
            jax.ShapeDtypeStruct((1, 256), F32),
        ),
        in_specs=[hbm] * 8,
        out_specs=(hbm, vmem, vmem),
        scratch_shapes=[
            pltpu.VMEM((count, 128, 128), F32),
            pltpu.VMEM((count, 128, 128), F32),
            pltpu.VMEM((128, 256), F32),
            pltpu.VMEM((128, 256), F32),
            pltpu.VMEM((nrep, 128, 128), F32),
            pltpu.VMEM((2, 128, 128), F32),
            pltpu.VMEM((nrep, 128, 128), F32),
            pltpu.VMEM((128, 256), F32),
            pltpu.VMEM((nplane, 8, 128), F32),
            pltpu.VMEM((nplane, 8, 128), F32),
            pltpu.VMEM((8, 128), F32),
            pltpu.VMEM((nz, 8, 128), F32),
            pltpu.VMEM((8, 128), F32),
            pltpu.VMEM((nplane, 8, 128), F32),
            pltpu.VMEM((8, 128), F32),
            pltpu.VMEM((nplane, 8, 128), F32),
            pltpu.VMEM((8, 128), F32),
            pltpu.VMEM((nz, 8, 128), F32),
            pltpu.VMEM((8, 128), F32),
            pltpu.VMEM((8, 128), F32),
            pltpu.SMEM((1, count), jnp.int32),
            pltpu.SMEM((1, count), jnp.int32),
            pltpu.VMEM((1, 256), F32),
            pltpu.VMEM((1, 128), jnp.int32),
            pltpu.SemaphoreType.REGULAR((2,)),
            dma((7,)),
            dma,
            dma,
            dma((count, CHUNKS)),
            dma,
            dma,
            dma((3,)),
            dma((3,)),
            dma((3,)),
            dma((3,)),
            dma((1,)),
        ],
        compiler_params=pltpu.CompilerParams(
            collective_id=0, has_side_effects=True, vmem_limit_bytes=24 * 1024 * 1024
        ),
    )(
        *(
            pltpu.with_memory_space_constraint(x, pltpu.HBM)
            for x in (
                features,
                weight,
                bias.reshape(1, 256),
                adjacency.reshape(count, 128, 128),
                tile_row.reshape(1, count),
                tile_live.reshape(1, count),
                node_live.reshape(1, 128),
                cotangent,
            )
        )
    )
    return write_out(act, wg, bg)


def solution(mesh):
    placed = (
        P(("row", "rep"), None),
        P(),
        P(),
        P("row", "rep", None, None, None),
        P("row", "rep", None),
        P("row", "rep", None),
        P(("row", "rep")),
        P(("row", "rep"), None),
    )
    return jax.shard_map(
        local,
        mesh=mesh,
        in_specs=placed,
        out_specs=(P(("row", "rep"), None), P(), P()),
        check_vma=False,
    )
```

time: 84.7 us -> 72.9 us (0.86)
  local copies, waits for them, and re-layouts: 9.35 us -> 0 us
  Pallas kernels: 74.4 us -> 72.1 us
    unnamed x19 -> x0, local copies, waits for them, and re-layouts: 9.35 us -> none
    pallas_call x1, Pallas kernels: 74.4 us -> 71.4 us  [local(): pl.pallas_call(kernel, out_shape=(jax.ShapeDtypeStruct((128, 256), F32),...]
where the time goes in v2:
time: 72.9 us; the launch traced here: 72.8 us
  Pallas kernels  72.1 us (99%)
    pallas_call x1, Pallas kernels, local(): pl.pallas_call(kernel, out_shape=(jax.ShapeDtypeStruct((128, 256), F32),...  71.4 us

profile of v2, /device:TPU:1, one launch (start us, length us, event | category | flops | bytes accessed | tf_op | source)
XLA Modules:
  0.0 72.8 jit_solution(12316758159455760962)
XLA Ops:
  0.6 71.4 %shard_map.103 = (f32[128,256]{1,0:T(8,128)S(1)}, f32[128,256]{1,0:T(8,128)S(1)}, f32[1,256]{1,0:T(1,128)S(1)}) custom-call(f32[128,128]{1,0:T(8,128)} %feat.1, f32[128,256]{1,0:T(8,128)} %weight.1, f32[1,256]{1,0:T(1,128)} %bitcast.7, f32[64,128,128]{2,1,0:T(8,128)} %bitcast.6, s32[1,64]{1,0:T(1,128)} %bitcast.8, s32[1,64]{1,0:T(1,128)} %bitcast.9, ...), custom_call_target="tpu_custom_call" | custom-call | tf_op jit(solution)/shard_map/pallas_call | solution.py:471
  72.0 0.7 %shard_map.104 = (f32[128,256]{1,0:T(8,128)}, f32[128,256]{1,0:T(8,128)}, f32[1,256]{1,0:T(1,128)}) custom-call(f32[128,256]{1,0:T(8,128)S(1)} %get-tuple-element.9.act, f32[128,256]{1,0:T(8,128)S(1)} %get-tuple-element.10.wg, f32[1,256]{1,0:T(1,128)S(1)} %get-tuple-element.11.bg), custom_call_target="tpu_custom_call" | custom-call | tf_op jit(solution)/shard_map/pallas_call | solution.py:452

commit v3 on v2

--- a/solution.py
+++ b/solution.py
@@ -256,11 +256,11 @@
     duo(7, h)
     take_all(block(slab(8), h, other))
     pair(slab(8), h)
-    duo(4, 1 - h)
+    for t in (4, 3, 6, 5):
+        duo(t, 1 - h)
     crossed(8)
     crossed(7)
-    for t in (3, 6, 5, 7):
-        duo(t, 1 - h)
+    duo(7, 1 - h)
     take_all(block(slab(8), 1 - h, other))
     pair(slab(8), 1 - h)
 

time: 72.9 us -> 71.9 us (0.986)
  Pallas kernels: 72.1 us -> 71.2 us
    pallas_call x1, Pallas kernels: 71.4 us -> 70.4 us  [local(): pl.pallas_call(kernel, out_shape=(jax.ShapeDtypeStruct((128, 256), F32),...]
where the time goes in v3:
time: 71.9 us; the launch traced here: 71.8 us
  Pallas kernels  71.2 us (99%)
    pallas_call x1, Pallas kernels, local(): pl.pallas_call(kernel, out_shape=(jax.ShapeDtypeStruct((128, 256), F32),...  70.4 us

profile of v3, /device:TPU:1, one launch (start us, length us, event | category | flops | bytes accessed | tf_op | source)
XLA Modules:
  0.0 71.8 jit_solution(16360599269407087915)
XLA Ops:
  0.6 70.4 %shard_map.103 = (f32[128,256]{1,0:T(8,128)S(1)}, f32[128,256]{1,0:T(8,128)S(1)}, f32[1,256]{1,0:T(1,128)S(1)}) custom-call(f32[128,128]{1,0:T(8,128)} %feat.1, f32[128,256]{1,0:T(8,128)} %weight.1, f32[1,256]{1,0:T(1,128)} %bitcast.7, f32[64,128,128]{2,1,0:T(8,128)} %bitcast.6, s32[1,64]{1,0:T(1,128)} %bitcast.8, s32[1,64]{1,0:T(1,128)} %bitcast.9, ...), custom_call_target="tpu_custom_call" | custom-call | tf_op jit(solution)/shard_map/pallas_call | solution.py:471
  71.1 0.7 %shard_map.104 = (f32[128,256]{1,0:T(8,128)}, f32[128,256]{1,0:T(8,128)}, f32[1,256]{1,0:T(1,128)}) custom-call(f32[128,256]{1,0:T(8,128)S(1)} %get-tuple-element.9.act, f32[128,256]{1,0:T(8,128)S(1)} %get-tuple-element.10.wg, f32[1,256]{1,0:T(1,128)S(1)} %get-tuple-element.11.bg), custom_call_target="tpu_custom_call" | custom-call | tf_op jit(solution)/shard_map/pallas_call | solution.py:452

commit v4 on v3

--- a/solution.py
+++ b/solution.py
@@ -163,7 +163,7 @@
         for c in range(CHUNKS):
             take(slot, c)
 
-    def pair(zz, hh):
+    def multiply(zz, hh):
         base = zz * 4 + hh * 2
         for j in range(2):
             fh, fl = split(gathered[base + j])
@@ -173,13 +173,16 @@
             left = jnp.concatenate([ah, al], axis=1)
             both = jnp.dot(left, right, preferred_element_type=F32)
             prods[j] = both[:, :128] + both[:, 128:]
-        picks = []
-        for j in range(2):
-            live = live_s[0, base + j].astype(F32)
-            target = row_s[0, base + j]
-            picks.append([jnp.where(target == a, live, 0.0) for a in range(8)])
+        return [(row_s[0, base + j], live_s[0, base + j].astype(F32)) for j in range(2)]
+
+    def add(rules, a):
+        picks = [jnp.where(target == a, live, 0.0) for target, live in rules]
+        acc[a] = acc[a] + (prods[0] * picks[0] + prods[1] * picks[1])
+
+    def pair(zz, hh):
+        rules = multiply(zz, hh)
         for a in range(8):
-            acc[a] = acc[a] + (prods[0] * picks[0][a] + prods[1] * picks[1][a])
+            add(rules, a)
 
     def duo(t, hh):
         for kk in range(2):
@@ -200,11 +203,11 @@
                     continue
                 slot = block(slab(-t), h, kk)
                 take(slot, c)
+                send(slot, c, across)
                 if t % 2 == 0:
                     for hop in (2, 1):
                         if t + hop <= end:
                             send(slot, c, ahead[hop])
-                send(slot, c, across)
                 send(slot, c, partner)
 
     def crossed(t):
@@ -260,21 +263,26 @@
         duo(t, 1 - h)
     crossed(8)
     crossed(7)
-    duo(7, 1 - h)
+    pair(slab(-7), 1 - h)
+    for kk in range(2):
+        take_all(block(slab(7), 1 - h, kk))
+    pair(slab(7), 1 - h)
     take_all(block(slab(8), 1 - h, other))
-    pair(slab(8), 1 - h)
 
     pl.semaphore_wait(ready.at[1], 2)
+    last = multiply(slab(8), 1 - h)
     for dy, dx in ((2, 1), (1, 1), (3, 1), (0, 1), (2, 0), (1, 0), (3, 0)):
         to = ((y + dy) % ny) * 2 + (side_x + dx) % 2
+        add(last, to)
         pltpu.make_async_remote_copy(
             src_ref=acc.at[to],
             dst_ref=incoming.at[dy * 2 + dx],
             send_sem=xs,
-            recv_sem=xr,
+            recv_sem=xr.at[dy * 2 + dx],
             device_id=at_device(row, to),
             device_id_type=MESH,
         ).start()
+    add(last, rep)
     w_copy.wait()
     c_copy.wait()
     bias_copy.wait()
@@ -282,9 +290,9 @@
     wh, wl = split(wv[...])
     live = jnp.transpose(jnp.broadcast_to(node_v[...].astype(F32), (128, 128)))
     mask = jnp.concatenate([live, live], axis=1)
-    arrived(incoming.at[pl.ds(1, nrep - 1)], xr)
     agg = acc[rep]
-    for j in range(1, nrep):
+    for j in (4, 2, 6, 1, 3, 7, 5):
+        arrived(incoming.at[j], xr.at[j])
         agg = agg + incoming[j]
     ah, al = split(agg)
     pre = jnp.dot(
@@ -508,7 +516,7 @@
             dma,
             dma((count, CHUNKS)),
             dma,
-            dma,
+            dma((nrep,)),
             dma((3,)),
             dma((3,)),
             dma((3,)),

time: 71.9 us -> 72 us (level)
  no operation moved by 1% of the time
where the time goes in v4:
time: 72 us; the launch traced here: 71.9 us
  Pallas kernels  71.2 us (99%)
    pallas_call x1, Pallas kernels, local(): pl.pallas_call(kernel, out_shape=(jax.ShapeDtypeStruct((128, 256), F32),...  70.5 us

profile of v4, /device:TPU:1, one launch (start us, length us, event | category | flops | bytes accessed | tf_op | source)
XLA Modules:
  0.0 71.9 jit_solution(7730942003508444554)
XLA Ops:
  0.6 70.5 %shard_map.103 = (f32[128,256]{1,0:T(8,128)S(1)}, f32[128,256]{1,0:T(8,128)S(1)}, f32[1,256]{1,0:T(1,128)S(1)}) custom-call(f32[128,128]{1,0:T(8,128)} %feat.1, f32[128,256]{1,0:T(8,128)} %weight.1, f32[1,256]{1,0:T(1,128)} %bitcast.7, f32[64,128,128]{2,1,0:T(8,128)} %bitcast.6, s32[1,64]{1,0:T(1,128)} %bitcast.8, s32[1,64]{1,0:T(1,128)} %bitcast.9, ...), custom_call_target="tpu_custom_call" | custom-call | tf_op jit(solution)/shard_map/pallas_call | solution.py:479
  71.1 0.7 %shard_map.104 = (f32[128,256]{1,0:T(8,128)}, f32[128,256]{1,0:T(8,128)}, f32[1,256]{1,0:T(1,128)}) custom-call(f32[128,256]{1,0:T(8,128)S(1)} %get-tuple-element.9.act, f32[128,256]{1,0:T(8,128)S(1)} %get-tuple-element.10.wg, f32[1,256]{1,0:T(1,128)S(1)} %get-tuple-element.11.bg), custom_call_target="tpu_custom_call" | custom-call | tf_op jit(solution)/shard_map/pallas_call | solution.py:460

commit v5 on v3

--- a/solution.py
+++ b/solution.py
@@ -54,10 +54,6 @@
     wsum,
     bpart,
     bplane,
-    breduced,
-    bz,
-    bfinal,
-    bsum,
     row_s,
     live_s,
     bias_v,
@@ -362,76 +358,72 @@
     total = part[me]
     for j in range(1, nplane):
         total = total + plane_in[j]
-    reduced[...] = total
-    z_in[z] = total
-
-    for dev in z_peers():
-        copy_to(reduced, z_in.at[z], 1, dev)
+    reduced[1] = total
+    z_in[z, 1] = total
+
+    @pl.when(me != 0)
+    def _():
+        for dev in z_peers():
+            copy_to(reduced.at[1], z_in.at[z, 1], 1, dev)
 
     @pl.when(me == 0)
     def _():
         arrived(bplane.at[pl.ds(1, nplane - 1)], br.at[0])
-        btotal = bpart[...]
+        extra = bpart[...]
         for j in range(1, nplane):
-            btotal = btotal + bplane[j]
-        breduced[...] = btotal
-        bz[z] = btotal
-
-        def balong(j, carry):
-            zz = (z + j) % nz
-            bcopy(breduced, bz.at[z], 1, at_device(zz * 4 + row % 4, rep)).start()
-            return carry
-
-        lax.fori_loop(1, nz, balong, 0)
-
-    arrived(z_in.at[pl.ds(1, nz - 1)], ar.at[1])
-    total = z_in[0]
+            extra = extra + bplane[j]
+        reduced[0] = extra
+        z_in[z, 0] = extra
+        for dev in z_peers():
+            copy_to(reduced, z_in.at[z], 1, dev)
+
+    def z_done(sem):
+        @pl.when(me != 0)
+        def _():
+            arrived(plane_in.at[pl.ds(1, nz - 1)], sem)
+
+        @pl.when(me == 0)
+        def _():
+            arrived(z_in.at[pl.ds(1, nz - 1)], sem)
+
+    z_done(ar.at[1])
+    total = z_in[0, 1]
     for j in range(1, nz):
-        total = total + z_in[j]
-    final[...] = total
-    wsum[me] = total
-
-    for j, q, dev in plane_peers():
-        copy_to(final, wsum.at[me], 2, dev)
+        total = total + z_in[j, 1]
+    final[1] = total
+    wsum[me + 1] = total
+
+    @pl.when(me != 0)
+    def _():
+        for _, _, dev in plane_peers():
+            copy_to(final.at[1], wsum.at[me + 1], 2, dev)
+        arrived(wsum.at[pl.ds(0, nplane)], ar.at[2])
+        arrived(plane_in.at[pl.ds(1, nplane - 1)], as_.at[2])
+        arrived(bpart, bs.at[0])
 
     @pl.when(me == 0)
     def _():
-        arrived(bz.at[pl.ds(1, nz - 1)], br.at[1])
-        btotal = bz[0]
+        extra = z_in[0, 0]
         for j in range(1, nz):
-            btotal = btotal + bz[j]
-        bfinal[...] = btotal
-        bsum[...] = btotal
-
-        def bgather(j, carry):
-            bcopy(bfinal, bsum, 2, at_device(z * 4 + j // nrep, j % nrep)).start()
-            return carry
-
-        lax.fori_loop(1, nplane, bgather, 0)
-
-    arrived(wsum.at[pl.ds(1, nplane - 1)], ar.at[2])
-    wg_out[:, :128] = wsum[pl.ds(0, 16)].reshape(128, 128)
-    wg_out[:, 128:] = wsum[pl.ds(16, 16)].reshape(128, 128)
-
-    @pl.when(me != 0)
-    def _():
-        arrived(bsum, br.at[2])
-        arrived(bpart, bs.at[0])
-
-    bg_out[:, :128] = bsum[0:1]
-    bg_out[:, 128:] = bsum[1:2]
-
-    @pl.when(me == 0)
-    def _():
-        arrived(bz.at[pl.ds(1, nz - 1)], bs.at[1])
-        arrived(bplane.at[pl.ds(1, nplane - 1)], bs.at[2])
-
+            extra = extra + z_in[j, 0]
+        final[0] = extra
+        wsum[0] = extra
+        for _, _, dev in plane_peers():
+            copy_to(final, wsum.at[pl.ds(0, 2)], 2, dev)
+        arrived(plane_in.at[pl.ds(1, nplane - 1)], ar.at[2])
+        arrived(wsum.at[pl.ds(0, nplane - 1)], as_.at[2])
+        arrived(wsum.at[pl.ds(0, nplane - 1)], as_.at[2])
+
+    wg_out[:, :128] = wsum[pl.ds(1, 16)].reshape(128, 128)
+    wg_out[:, 128:] = wsum[pl.ds(17, 16)].reshape(128, 128)
+    bg_out[:, :128] = wsum[0, 0:1]
+    bg_out[:, 128:] = wsum[0, 1:2]
+
+    z_done(as_.at[1])
     sent = nz * 4 - 1
     arrived(gathered.at[pl.ds(0, sent)], ssem)
     arrived(incoming.at[pl.ds(1, nrep - 1)], xs)
     arrived(plane_in.at[pl.ds(1, nplane - 1)], as_.at[0])
-    arrived(z_in.at[pl.ds(1, nz - 1)], as_.at[1])
-    arrived(plane_in.at[pl.ds(1, nplane - 1)], as_.at[2])
     act_copy.wait()
 
 
@@ -488,16 +480,12 @@
             pltpu.VMEM((128, 256), F32),
             pltpu.VMEM((nplane, 8, 128), F32),
             pltpu.VMEM((nplane, 8, 128), F32),
-            pltpu.VMEM((8, 128), F32),
-            pltpu.VMEM((nz, 8, 128), F32),
+            pltpu.VMEM((2, 8, 128), F32),
+            pltpu.VMEM((nz, 2, 8, 128), F32),
+            pltpu.VMEM((2, 8, 128), F32),
+            pltpu.VMEM((nplane + 1, 8, 128), F32),
             pltpu.VMEM((8, 128), F32),
             pltpu.VMEM((nplane, 8, 128), F32),
-            pltpu.VMEM((8, 128), F32),
-            pltpu.VMEM((nplane, 8, 128), F32),
-            pltpu.VMEM((8, 128), F32),
-            pltpu.VMEM((nz, 8, 128), F32),
-            pltpu.VMEM((8, 128), F32),
-            pltpu.VMEM((8, 128), F32),
             pltpu.SMEM((1, count), jnp.int32),
             pltpu.SMEM((1, count), jnp.int32),
             pltpu.VMEM((1, 256), F32),
@@ -511,8 +499,8 @@
             dma,
             dma((3,)),
             dma((3,)),
-            dma((3,)),
-            dma((3,)),
+            dma((1,)),
+            dma((1,)),
             dma((1,)),
         ],
         compiler_params=pltpu.CompilerParams(

time: 71.9 us -> 71.8 us (level)
  no operation moved by 1% of the time
where the time goes in v5:
time: 71.8 us; the launch traced here: 71.7 us
  Pallas kernels  71.1 us (99%)
    pallas_call x1, Pallas kernels, local(): pl.pallas_call(kernel, out_shape=(jax.ShapeDtypeStruct((128, 256), F32),...  70.4 us

profile of v5, /device:TPU:1, one launch (start us, length us, event | category | flops | bytes accessed | tf_op | source)
XLA Modules:
  0.0 71.7 jit_solution(14821954774668618708)
XLA Ops:
  0.6 70.4 %shard_map.103 = (f32[128,256]{1,0:T(8,128)S(1)}, f32[128,256]{1,0:T(8,128)S(1)}, f32[1,256]{1,0:T(1,128)S(1)}) custom-call(f32[128,128]{1,0:T(8,128)} %feat.1, f32[128,256]{1,0:T(8,128)} %weight.1, f32[1,256]{1,0:T(1,128)} %bitcast.7, f32[64,128,128]{2,1,0:T(8,128)} %bitcast.6, s32[1,64]{1,0:T(1,128)} %bitcast.8, s32[1,64]{1,0:T(1,128)} %bitcast.9, ...), custom_call_target="tpu_custom_call" | custom-call | tf_op jit(solution)/shard_map/pallas_call | solution.py:463
  71.0 0.7 %shard_map.104 = (f32[128,256]{1,0:T(8,128)}, f32[128,256]{1,0:T(8,128)}, f32[1,256]{1,0:T(1,128)}) custom-call(f32[128,256]{1,0:T(8,128)S(1)} %get-tuple-element.9.act, f32[128,256]{1,0:T(8,128)S(1)} %get-tuple-element.10.wg, f32[1,256]{1,0:T(1,128)S(1)} %get-tuple-element.11.bg), custom_call_target="tpu_custom_call" | custom-call | tf_op jit(solution)/shard_map/pallas_call | solution.py:444
